TPU v7x, 256 devices: a whole 4x4x8 slice. The times are simulated.
256 devices in a mesh: samp: 64 (over z, x, core), snp: 4 (over y).
Axes of the slice: x: 4, y: 4, z: 8, core: 2. Of those that a mesh axis runs over, the one named last changes fastest.
Arguments:
- genotype: int32 [40960, 4096], P('samp', 'snp'), may hold values from 0 to 2
- freqs: float32 [4096], P('snp'), may hold values from 0.35 to 0.65
- left_factors: float32 [40960, 20], P('samp'), may hold values from -6 to 6
- singular: float32 [20], replicated, may hold values from 0.5 to 2
- right_factors: float32 [4096, 20], P(('snp', 'samp')), may hold values from -1.25 to 1.25
- sketch: bfloat16 [4096, 64], P('snp'), may hold values from -6 to 6
- batch_sizes: int32 [12], replicated, may hold values from 1 to 6826, 40960 in all
- missing_batch: int32 [48], replicated, may hold values from 0 to 11, as said below
- missing_block: int32 [48], replicated, may hold values from 0 to 15, as said below
Outputs:
- basis: float32 [40960, 64], P('samp')
- projection: float32 [4096, 64], P('snp')
- snp_basis: float32 [4096, 64], P('snp')
Inputs may be any that keep to these rules, and one draw needn't show every extreme that they name: The pairs (missing_batch, missing_block) are distinct; every block id appears exactly 3 times and every batch id exactly 48 // 12 times. `missing_block`: paired entry by entry with missing_batch.
All inputs are finite; a program needn't handle non-finite values.
Results may differ from a plain program's by a relative error of at most 0.012.
Values may be sent and summed in bfloat16 or wider, within the bound.
No kernel may reach another device: no remote copies, remote signals or barrier semaphores. Data moves between devices by JAX's collectives and lax.ppermute only.
A program may use at most 64 MiB of HBM per device.

v0:
```python
import math
import jax
import jax.numpy as jnp
from jax import lax
from jax.sharding import PartitionSpec as P

BATCHES = 12
BLOCK = 256
ITERS = 2
BLOCKS = 16


def finish_basis(values, gram):
    lower = jnp.linalg.cholesky(gram)
    return jax.scipy.linalg.solve_triangular(lower, values.T, lower=True).T


def reversed_basis(values, gram):
    flipped = finish_basis(values[:, ::-1], gram[::-1, ::-1])
    return flipped[:, ::-1]


def own_gram(values):
    return jnp.dot(values.T, values, precision=lax.Precision.HIGHEST)


def sample_basis(matrix, right_side, sample_count):
    partial_value = jnp.dot(matrix, right_side, preferred_element_type=jnp.float32)
    summed = lax.psum(partial_value.astype(jnp.bfloat16), "snp").astype(jnp.float32)
    gram = lax.psum(own_gram(summed), "samp") / sample_count
    return finish_basis(summed, gram)


def snp_columns(matrix, basis):
    local_part = lax.dot_general(
        matrix,
        basis.astype(jnp.bfloat16),
        (((0,), (0,)), ((), ())),
        preferred_element_type=jnp.float32,
    )
    return lax.psum(local_part, "samp")


def snp_basis(columns, snp_count):
    gram = lax.psum(own_gram(columns), "snp") / snp_count
    return reversed_basis(columns, gram)


def on_device(
    genotype,
    freqs,
    left_factors,
    singular,
    right_factors,
    sketch,
    batch_sizes,
    missing_batch,
    missing_block,
):
    row_count, col_width = genotype.shape
    sample_count = row_count * lax.axis_size("samp")
    snp_count = col_width * lax.axis_size("snp")
    right_local = lax.all_gather(right_factors, "samp", axis=0, tiled=True)
    batch_range = jnp.arange(BATCHES, dtype=jnp.int32)
    block_range = jnp.arange(BLOCKS, dtype=jnp.int32)
    hot_batch = (missing_batch[:, None] == batch_range[None, :]).astype(jnp.float32)
    hot_block = (missing_block[:, None] == block_range[None, :]).astype(jnp.float32)
    table = jnp.dot(hot_batch.T, hot_block, preferred_element_type=jnp.float32)
    ends = jnp.cumsum(batch_sizes)
    row_ids = lax.axis_index("samp") * row_count + jnp.arange(row_count, dtype=jnp.int32)
    batch_of = jnp.sum((row_ids[:, None] >= ends[None, :]).astype(jnp.int32), axis=1)
    row_hot = (batch_of[:, None] == batch_range[None, :]).astype(jnp.float32)
    col_ids = lax.axis_index("snp") * col_width + jnp.arange(col_width, dtype=jnp.int32)
    col_hot = ((col_ids // BLOCK)[None, :] == block_range[:, None]).astype(jnp.float32)
    missing = (
        jnp.dot(
            jnp.dot(row_hot, table, preferred_element_type=jnp.float32),
            col_hot,
            preferred_element_type=jnp.float32,
        )
        > 0.5
    )
    lowrank = jnp.dot(
        left_factors * singular[None, :], right_local.T, precision=lax.Precision.HIGHEST
    )
    observed = genotype.astype(jnp.float32) - 2.0 * freqs[None, :]
    matrix = jnp.where(missing, lowrank, observed).astype(jnp.bfloat16)
    basis = sample_basis(matrix, sketch, sample_count)
    column_basis = jnp.zeros((col_width, sketch.shape[1]), jnp.float32)
    for sweep_index in range(ITERS):
        column_basis = snp_basis(snp_columns(matrix, basis), snp_count)
        basis = sample_basis(matrix, column_basis.astype(jnp.bfloat16), sample_count)
    projection = snp_columns(matrix, basis) / math.sqrt(sample_count)
    return (basis, projection, column_basis)


def solution(mesh):
    in_specs = (
        P("samp", "snp"),
        P("snp"),
        P("samp", None),
        P(),
        P(("snp", "samp"), None),
        P("snp", None),
        P(),
        P(),
        P(),
    )
    out_specs = (P("samp", None), P("snp", None), P("snp", None))
    return jax.shard_map(
        on_device, mesh=mesh, in_specs=in_specs, out_specs=out_specs, check_vma=False
    )
```

profile of v0, /device:TPU:1, one launch (start us, length us, event | category | flops | bytes accessed | tf_op | source)
XLA Modules:
  0.0 1585.5 jit_solution(2528023982231809789)
XLA Ops:
  8.0 54.6 %all_gather.3 = f32[1024,20]{1,0:T(8,128)S(1)} all-gather(f32[16,20]{1,0:T(8,128)} %param.18), channel_id=1, replica_groups=mesh['samp'=64,'snp'=4] {'samp'}, dimensions={0}, use_global_device_ids=true | all-gather | bytes 83200 | tf_op jit(solution)/shard_map/all_gather | solution.py:63
  66.6 5.1 select_convert_fusion
  72.9 40.8 %all-reduce.7.cloned.1.call-done = bf16[640,64]{0,1:T(8,128)(2,1)} async-done(((bf16[640,64]{0,1:T(8,128)(2,1)}), bf16[640,64]{0,1:T(8,128)(2,1)}) %all-reduce.7.cloned.1.call-update) | async-done | bytes 81936 | tf_op jit(solution)/shard_map/psum | solution.py:29
  114.8 246.0 %psum.78 = f32[64,64]{0,1:T(8,128)S(1)} all-reduce(f32[64,64]{0,1:T(8,128)S(1)} %fusion.49), channel_id=1, replica_groups=mesh['samp'=64,'snp'=4] {'samp'}, use_global_device_ids=true, to_apply=%region_3.4 | all-reduce | flops 4096 | bytes 32768 | tf_op jit(solution)/shard_map/psum | solution.py:30
  360.9 5.8 cholesky.89
  368.1 4.9 custom-call.11
  375.4 176.2 %all-reduce.9.cloned.1.call-done = f32[1024,64]{0,1:T(8,128)} async-done(((f32[1024,64]{0,1:T(8,128)}), f32[1024,64]{0,1:T(8,128)}) %all-reduce.9.cloned.1.call-update) | async-done | bytes 262160 | tf_op jit(solution)/shard_map/psum | solution.py:41
  553.1 13.3 psum.80
  566.5 5.8 cholesky.100
  573.7 4.9 custom-call.12
  583.7 42.7 %all-reduce.11.cloned.1.call-done = bf16[640,64]{0,1:T(8,128)(2,1)} async-done(((bf16[640,64]{0,1:T(8,128)(2,1)}), bf16[640,64]{0,1:T(8,128)(2,1)}) %all-reduce.11.cloned.1.call-update) | async-done | bytes 81936 | tf_op jit(solution)/shard_map/psum | solution.py:29
  627.5 246.0 %psum.82 = f32[64,64]{0,1:T(8,128)S(1)} all-reduce(f32[64,64]{0,1:T(8,128)S(1)} %fusion.51), channel_id=1, replica_groups=mesh['samp'=64,'snp'=4] {'samp'}, use_global_device_ids=true, to_apply=%region_9.13 | all-reduce | flops 4096 | bytes 32768 | tf_op jit(solution)/shard_map/psum | solution.py:30
  873.6 5.8 cholesky.111
  880.8 4.9 custom-call.13
  888.1 176.2 %all-reduce.13.cloned.1.call-done = f32[1024,64]{0,1:T(8,128)} async-done(((f32[1024,64]{0,1:T(8,128)}), f32[1024,64]{0,1:T(8,128)}) %all-reduce.13.cloned.1.call-update) | async-done | bytes 262160 | tf_op jit(solution)/shard_map/psum | solution.py:41
  1065.8 13.3 psum.84
  1079.2 5.8 cholesky.122
  1086.4 4.9 custom-call.14
  1091.3 3.1 rev.22
  1096.2 42.8 %all-reduce.15.cloned.1.call-done = bf16[640,64]{0,1:T(8,128)(2,1)} async-done(((bf16[640,64]{0,1:T(8,128)(2,1)}), bf16[640,64]{0,1:T(8,128)(2,1)}) %all-reduce.15.cloned.1.call-update) | async-done | bytes 81936 | tf_op jit(solution)/shard_map/psum | solution.py:29
  1140.2 246.0 %psum.86 = f32[64,64]{0,1:T(8,128)S(1)} all-reduce(f32[64,64]{0,1:T(8,128)S(1)} %fusion.53), channel_id=1, replica_groups=mesh['samp'=64,'snp'=4] {'samp'}, use_global_device_ids=true, to_apply=%region_13.17 | all-reduce | flops 4096 | bytes 32768 | tf_op jit(solution)/shard_map/psum | solution.py:30
  1386.3 5.8 cholesky.133
  1393.5 4.9 custom-call.15
  1400.7 176.2 %all-reduce.17.cloned.1.call-done = f32[1024,64]{0,1:T(8,128)} async-done(((f32[1024,64]{0,1:T(8,128)}), f32[1024,64]{0,1:T(8,128)}) %all-reduce.17.cloned.1.call-update) | async-done | bytes 262160 | tf_op jit(solution)/shard_map/psum | solution.py:41
  (81 shorter events, 35.0 us)
Async XLA Ops:
  7.2 64.5 %copy-start = (bf16[1024,64]{0,1:T(8,128)(2,1)S(1)}, bf16[1024,64]{0,1:T(8,128)(2,1)}, u32[]{:S(2)}) copy-start(bf16[1024,64]{0,1:T(8,128)(2,1)} %param.19) | copy-start | bytes 393220
  7.2 106.5 %all-reduce.7.cloned.1.call-start = ((), (), s32[]{:S(2)}) async-start(), calls=%async_computation | async-start | bytes 163840 | tf_op jit(solution)/shard_map/psum | solution.py:29
  64.4 2.2 copy-start.3
  64.4 2.2 copy-start.4
  72.9 478.7 %all-reduce.9.cloned.1.call-start = ((), (), s32[]{:S(2)}) async-start(), calls=%async_computation.1 | async-start | bytes 524288 | tf_op jit(solution)/shard_map/psum | solution.py:41
  375.3 251.1 %all-reduce.11.cloned.1.call-start = ((), (), s32[]{:S(2)}) async-start(), calls=%async_computation.2 | async-start | bytes 163840 | tf_op jit(solution)/shard_map/psum | solution.py:29
  583.5 480.8 %all-reduce.13.cloned.1.call-start = ((), (), s32[]{:S(2)}) async-start(), calls=%async_computation.3 | async-start | bytes 524288 | tf_op jit(solution)/shard_map/psum | solution.py:41
  888.0 251.0 %all-reduce.15.cloned.1.call-start = ((), (), s32[]{:S(2)}) async-start(), calls=%async_computation.4 | async-start | bytes 163840 | tf_op jit(solution)/shard_map/psum | solution.py:29
  1095.0 305.7 %copy-start.1 = (f32[1024,64]{0,1:T(8,128)}, f32[1024,64]{0,1:T(8,128)S(1)}, u32[]{:S(2)}) copy-start(f32[1024,64]{0,1:T(8,128)S(1)} %rev.23) | copy-start | bytes 786436
  1096.2 480.8 %all-reduce.17.cloned.1.call-start = ((), (), s32[]{:S(2)}) async-start(), calls=%async_computation.5 | async-start | bytes 524288 | tf_op jit(solution)/shard_map/psum | solution.py:41
  1399.6 179.0 %copy-start.2 = (f32[640,64]{0,1:T(8,128)}, f32[640,64]{0,1:T(8,128)S(1)}, u32[]{:S(2)}) copy-start(f32[640,64]{0,1:T(8,128)S(1)} %convolution_bitcast_fusion.2) | copy-start | bytes 491524
Sparse Core Ops, SparseCore 0:
  73.0 40.6 all-reduce.6
  375.5 176.0 all-reduce.8
  583.6 42.7 all-reduce.10
  888.2 176.1 all-reduce.12
  1096.3 42.7 all-reduce.14
  1400.8 176.0 all-reduce.16
where the time goes:
time: 1590 us
  blocking collectives  819 us (52%)
  waiting for transfers between devices  655 us (41%)
  other arithmetic  63.7 us (4%)
  matrix products  25.5 us (2%)
    psum x3, blocking collectives, sample_basis(): gram = lax.psum(own_gram(summed), 'samp') / sample_count  738 us
    psum x3, waiting for transfers between devices, snp_columns(): return lax.psum(local_part, 'samp')  529 us
    psum x3, waiting for transfers between devices, sample_basis(): lax.psum(partial_value.astype(jnp.bfloat16), 'snp').astype(jnp.float32)  126 us
    all_gather x1, blocking collectives, on_device(): right_local = lax.all_gather(right_factors, 'samp', axis=0, tiled=True)  54.6 us
    another operation x15, other arithmetic, finish_basis(): lower = jnp.linalg.cholesky(gram)  32.6 us
  transfers between devices with their start and end apart: 6, of which 6 were waited for; matrix products, arithmetic and copies ran while one was open for 0% of the time, Pallas kernels for 0%

commit v1 on v0

--- a/solution.py
+++ b/solution.py
@@ -38,7 +38,7 @@
         (((0,), (0,)), ((), ())),
         preferred_element_type=jnp.float32,
     )
-    return lax.psum(local_part, "samp")
+    return jnp.sum(lax.all_gather(local_part, "samp"), axis=0)
 
 
 def snp_basis(columns, snp_count):

time: 1590 us -> 1440 us (0.906)
  waiting for transfers between devices: 655 us -> 427 us
  local copies, waits for them, and re-layouts: 7.18 us -> 54.4 us
  other arithmetic: 63.7 us -> 88.2 us
    psum x3 -> x0, waiting for transfers between devices: 529 us -> none  [snp_columns(): return lax.psum(local_part, 'samp')]
    all_gather x0 -> x3, waiting for transfers between devices: none -> 302 us  [snp_columns(): return jnp.sum(lax.all_gather(local_part, 'samp'), axis=0)]
    unnamed x10 -> x15, local copies, waits for them, and re-layouts: 0.03 us -> 53.1 us
    reduce_sum x0 -> x3, other arithmetic: none -> 25.4 us  [snp_columns(): return jnp.sum(lax.all_gather(local_part, 'samp'), axis=0)]
where the time goes in v1:
time: 1440 us; the launch traced here: 1430 us
  blocking collectives  819 us (57%)
  waiting for transfers between devices  427 us (30%)
  other arithmetic  88.2 us (6%)
  local copies, waits for them, and re-layouts  54.4 us (4%)
  matrix products  23.5 us (2%)
  between operations  14.7 us (1%)
    psum x3, blocking collectives, sample_basis(): gram = lax.psum(own_gram(summed), 'samp') / sample_count  738 us
    all_gather x3, waiting for transfers between devices, snp_columns(): return jnp.sum(lax.all_gather(local_part, 'samp'), axis=0)  302 us
    psum x3, waiting for transfers between devices, sample_basis(): lax.psum(partial_value.astype(jnp.bfloat16), 'snp').astype(jnp.float32)  125 us
    all_gather x1, blocking collectives, on_device(): right_local = lax.all_gather(right_factors, 'samp', axis=0, tiled=True)  54.6 us
    unnamed x15, local copies, waits for them, and re-layouts  53.1 us
    another operation x15, other arithmetic, finish_basis(): lower = jnp.linalg.cholesky(gram)  32.6 us
  transfers between devices with their start and end apart: 6, of which 6 were waited for; matrix products, arithmetic and copies ran while one was open for 0% of the time, Pallas kernels for 0%

profile of v1, /device:TPU:1, one launch (start us, length us, event | category | flops | bytes accessed | tf_op | source)
XLA Modules:
  0.0 1428.2 jit_solution(2491156806354644555)
XLA Ops:
  8.0 54.6 %all_gather.21 = f32[1024,20]{1,0:T(8,128)S(1)} all-gather(f32[16,20]{1,0:T(8,128)} %param.18), channel_id=1, replica_groups=mesh['samp'=64,'snp'=4] {'samp'}, dimensions={0}, use_global_device_ids=true | all-gather | bytes 83200 | tf_op jit(solution)/shard_map/all_gather | solution.py:63
  66.7 5.1 select_convert_fusion
  73.1 40.8 %all-reduce.4.cloned.1.call-done = bf16[640,64]{0,1:T(8,128)(2,1)} async-done(((bf16[640,64]{0,1:T(8,128)(2,1)}), bf16[640,64]{0,1:T(8,128)(2,1)}) %all-reduce.4.cloned.1.call-update) | async-done | bytes 81936 | tf_op jit(solution)/shard_map/psum | solution.py:29
  114.9 246.0 %psum.57 = f32[64,64]{0,1:T(8,128)S(1)} all-reduce(f32[64,64]{0,1:T(8,128)S(1)} %fusion.49), channel_id=1, replica_groups=mesh['samp'=64,'snp'=4] {'samp'}, use_global_device_ids=true, to_apply=%region_3.4 | all-reduce | flops 4096 | bytes 32768 | tf_op jit(solution)/shard_map/psum | solution.py:30
  361.0 5.8 cholesky.89
  376.0 100.3 %all-gather.7.cloned.1.call-done = f32[65536,64]{0,1:T(8,128)} async-done(((f32[1024,64]{0,1:T(8,128)}), f32[65536,64]{0,1:T(8,128)}) %all-gather.7.cloned.1.call-update) | async-done | bytes 16777232 | tf_op jit(solution)/shard_map/all_gather | solution.py:41
  476.3 17.7 %copy.47 = f32[8,8,64,1024]{3,2,1,0:T(8,128)} copy(f32[8,8,64,1024]{3,1,2,0:T(8,128)} %bitcast.105) | data formatting | bytes 33554432
  493.9 8.5 bitcast_reduce_fusion.2
  503.1 13.3 psum.58
  516.5 5.8 cholesky.100
  530.5 42.3 %all-reduce.6.cloned.1.call-done = bf16[640,64]{0,1:T(8,128)(2,1)} async-done(((bf16[640,64]{0,1:T(8,128)(2,1)}), bf16[640,64]{0,1:T(8,128)(2,1)}) %all-reduce.6.cloned.1.call-update) | async-done | bytes 81936 | tf_op jit(solution)/shard_map/psum | solution.py:29
  573.8 246.0 %psum.60 = f32[64,64]{0,1:T(8,128)S(1)} all-reduce(f32[64,64]{0,1:T(8,128)S(1)} %fusion.51), channel_id=1, replica_groups=mesh['samp'=64,'snp'=4] {'samp'}, use_global_device_ids=true, to_apply=%region_9.13 | all-reduce | flops 4096 | bytes 32768 | tf_op jit(solution)/shard_map/psum | solution.py:30
  820.0 5.8 cholesky.111
  834.6 100.6 %all-gather.9.cloned.1.call-done = f32[65536,64]{0,1:T(8,128)} async-done(((f32[1024,64]{0,1:T(8,128)}), f32[65536,64]{0,1:T(8,128)}) %all-gather.9.cloned.1.call-update) | async-done | bytes 16777232 | tf_op jit(solution)/shard_map/all_gather | solution.py:41
  935.2 17.7 %copy.48 = f32[8,8,64,1024]{3,2,1,0:T(8,128)} copy(f32[8,8,64,1024]{3,1,2,0:T(8,128)} %bitcast.106) | data formatting | bytes 33554432
  952.8 8.5 bitcast_reduce_fusion.1
  962.0 13.3 psum.61
  975.4 5.8 cholesky.122
  989.3 42.3 %all-reduce.8.cloned.1.call-done = bf16[640,64]{0,1:T(8,128)(2,1)} async-done(((bf16[640,64]{0,1:T(8,128)(2,1)}), bf16[640,64]{0,1:T(8,128)(2,1)}) %all-reduce.8.cloned.1.call-update) | async-done | bytes 81936 | tf_op jit(solution)/shard_map/psum | solution.py:29
  1032.7 246.2 %psum.63 = f32[64,64]{0,1:T(8,128)S(1)} all-reduce(f32[64,64]{0,1:T(8,128)S(1)} %fusion.53), channel_id=1, replica_groups=mesh['samp'=64,'snp'=4] {'samp'}, use_global_device_ids=true, to_apply=%region_13.17 | all-reduce | flops 4096 | bytes 32768 | tf_op jit(solution)/shard_map/psum | solution.py:30
  1279.0 5.8 cholesky.133
  1293.4 100.8 %all-gather.11.cloned.1.call-done = f32[65536,64]{0,1:T(8,128)} async-done(((f32[1024,64]{0,1:T(8,128)}), f32[65536,64]{0,1:T(8,128)}) %all-gather.11.cloned.1.call-update) | async-done | bytes 16777232 | tf_op jit(solution)/shard_map/all_gather | solution.py:41
  1394.2 17.7 %copy.49 = f32[8,8,64,1024]{3,2,1,0:T(8,128)} copy(f32[8,8,64,1024]{3,1,2,0:T(8,128)} %bitcast.107) | data formatting | bytes 33554432
  1411.9 8.5 bitcast_reduce_fusion
  (89 shorter events, 54.4 us)
Async XLA Ops:
  7.2 64.7 %copy-start = (bf16[1024,64]{0,1:T(8,128)(2,1)S(1)}, bf16[1024,64]{0,1:T(8,128)(2,1)}, u32[]{:S(2)}) copy-start(bf16[1024,64]{0,1:T(8,128)(2,1)} %param.19) | copy-start | bytes 393220
  7.2 59.5 %copy-start.5 = (f32[20]{0:T(128)S(1)}, f32[20]{0:T(128)}, u32[]{:S(2)}) copy-start(f32[20]{0:T(128)} %param.17) | copy-start | bytes 244
  7.2 59.5 %copy-start.4 = (f32[640,20]{0,1:T(8,128)S(1)}, f32[640,20]{0,1:T(8,128)}, u32[]{:S(2)}) copy-start(f32[640,20]{0,1:T(8,128)} %param.16) | copy-start | bytes 153604
  7.2 106.6 %all-reduce.4.cloned.1.call-start = ((), (), s32[]{:S(2)}) async-start(), calls=%async_computation | async-start | bytes 163840 | tf_op jit(solution)/shard_map/psum | solution.py:29
  73.0 403.2 %all-gather.7.cloned.1.call-start = ((), (), s32[]{:S(2)}) async-start(), calls=%async_computation.3 | async-start | bytes 17039360 | tf_op jit(solution)/shard_map/all_gather | solution.py:41
  375.5 197.3 %all-reduce.6.cloned.1.call-start = ((), (), s32[]{:S(2)}) async-start(), calls=%async_computation.1 | async-start | bytes 163840 | tf_op jit(solution)/shard_map/psum | solution.py:29
  530.4 404.8 %all-gather.9.cloned.1.call-start = ((), (), s32[]{:S(2)}) async-start(), calls=%async_computation.4 | async-start | bytes 17039360 | tf_op jit(solution)/shard_map/all_gather | solution.py:41
  834.4 197.2 %all-reduce.8.cloned.1.call-start = ((), (), s32[]{:S(2)}) async-start(), calls=%async_computation.2 | async-start | bytes 163840 | tf_op jit(solution)/shard_map/psum | solution.py:29
  988.1 423.8 %copy-start.2 = (f32[1024,64]{0,1:T(8,128)}, f32[1024,64]{0,1:T(8,128)S(1)}, u32[]{:S(2)}) copy-start(f32[1024,64]{0,1:T(8,128)S(1)} %rev.23) | copy-start | bytes 786436
  989.3 405.0 %all-gather.11.cloned.1.call-start = ((), (), s32[]{:S(2)}) async-start(), calls=%async_computation.5 | async-start | bytes 17039360 | tf_op jit(solution)/shard_map/all_gather | solution.py:41
  1292.3 119.6 %copy-start.3 = (f32[640,64]{0,1:T(8,128)}, f32[640,64]{0,1:T(8,128)S(1)}, u32[]{:S(2)}) copy-start(f32[640,64]{0,1:T(8,128)S(1)} %convolution_bitcast_fusion.2) | copy-start | bytes 491524
  1411.9 9.2 copy-start.1
Sparse Core Ops, SparseCore 0:
  73.1 40.6 all-reduce.3
  375.6 100.6 all-gather.6
  530.5 42.1 all-reduce.5
  834.5 100.6 all-gather.8
  989.4 42.1 all-reduce.7
  1293.6 100.6 all-gather.10

commit v2 on v0

--- a/solution.py
+++ b/solution.py
@@ -60,7 +60,9 @@
     row_count, col_width = genotype.shape
     sample_count = row_count * lax.axis_size("samp")
     snp_count = col_width * lax.axis_size("snp")
-    right_local = lax.all_gather(right_factors, "samp", axis=0, tiled=True)
+    right_local = jnp.concatenate(
+        lax.all_to_all(jnp.stack([right_factors] * lax.axis_size("samp")), "samp", 0, 0), axis=0
+    )
     batch_range = jnp.arange(BATCHES, dtype=jnp.int32)
     block_range = jnp.arange(BLOCKS, dtype=jnp.int32)
     hot_batch = (missing_batch[:, None] == batch_range[None, :]).astype(jnp.float32)

time: 1590 us -> 1550 us (0.975)
  blocking collectives: 819 us -> 765 us
    all_gather x1 -> x0, blocking collectives: 54.6 us -> none  [on_device(): right_local = lax.all_gather(right_factors, 'samp', axis=0, tiled=True)]
  transfers between devices with their start and end apart: 6 -> 7, of which waited for: 6 -> 7; matrix products, arithmetic and copies ran while one was open for 0% -> 0% of each run, Pallas kernels for 0% -> 0%
where the time goes in v2:
time: 1550 us
  blocking collectives  765 us (49%)
  waiting for transfers between devices  660 us (43%)
  other arithmetic  63.3 us (4%)
  matrix products  24.8 us (2%)
    psum x3, blocking collectives, sample_basis(): gram = lax.psum(own_gram(summed), 'samp') / sample_count  738 us
    psum x3, waiting for transfers between devices, snp_columns(): return lax.psum(local_part, 'samp')  529 us
    psum x3, waiting for transfers between devices, sample_basis(): lax.psum(partial_value.astype(jnp.bfloat16), 'snp').astype(jnp.float32)  124 us
    another operation x15, other arithmetic, finish_basis(): lower = jnp.linalg.cholesky(gram)  32.6 us
  transfers between devices with their start and end apart: 7, of which 7 were waited for; matrix products, arithmetic and copies ran while one was open for 0% of the time, Pallas kernels for 0%

profile of v2, /device:TPU:1, one launch (start us, length us, event | category | flops | bytes accessed | tf_op | source)
XLA Modules:
  0.0 1550.6 jit_solution(9244555907349203321)
XLA Ops:
  9.0 13.0 all-to-all-start
  24.8 7.7 all-to-all-done
  34.3 5.1 select_convert_fusion
  40.6 38.2 %all-reduce.7.cloned.1.call-done = bf16[640,64]{0,1:T(8,128)(2,1)} async-done(((bf16[640,64]{0,1:T(8,128)(2,1)}), bf16[640,64]{0,1:T(8,128)(2,1)}) %all-reduce.7.cloned.1.call-update) | async-done | bytes 81936 | tf_op jit(solution)/shard_map/psum | solution.py:29
  79.9 246.0 %psum.78 = f32[64,64]{0,1:T(8,128)S(1)} all-reduce(f32[64,64]{0,1:T(8,128)S(1)} %fusion.49), channel_id=1, replica_groups=mesh['samp'=64,'snp'=4] {'samp'}, use_global_device_ids=true, to_apply=%region_3.4 | all-reduce | flops 4096 | bytes 32768 | tf_op jit(solution)/shard_map/psum | solution.py:30
  326.0 5.8 cholesky.89
  333.2 4.9 custom-call.11
  340.5 176.1 %all-reduce.9.cloned.1.call-done = f32[1024,64]{0,1:T(8,128)} async-done(((f32[1024,64]{0,1:T(8,128)}), f32[1024,64]{0,1:T(8,128)}) %all-reduce.9.cloned.1.call-update) | async-done | bytes 262160 | tf_op jit(solution)/shard_map/psum | solution.py:41
  518.1 13.3 psum.80
  531.5 5.8 cholesky.100
  538.7 4.9 custom-call.12
  548.6 42.8 %all-reduce.11.cloned.1.call-done = bf16[640,64]{0,1:T(8,128)(2,1)} async-done(((bf16[640,64]{0,1:T(8,128)(2,1)}), bf16[640,64]{0,1:T(8,128)(2,1)}) %all-reduce.11.cloned.1.call-update) | async-done | bytes 81936 | tf_op jit(solution)/shard_map/psum | solution.py:29
  592.5 246.2 %psum.82 = f32[64,64]{0,1:T(8,128)S(1)} all-reduce(f32[64,64]{0,1:T(8,128)S(1)} %fusion.51), channel_id=1, replica_groups=mesh['samp'=64,'snp'=4] {'samp'}, use_global_device_ids=true, to_apply=%region_9.13 | all-reduce | flops 4096 | bytes 32768 | tf_op jit(solution)/shard_map/psum | solution.py:30
  838.8 5.8 cholesky.111
  846.0 4.9 custom-call.13
  853.3 176.2 %all-reduce.13.cloned.1.call-done = f32[1024,64]{0,1:T(8,128)} async-done(((f32[1024,64]{0,1:T(8,128)}), f32[1024,64]{0,1:T(8,128)}) %all-reduce.13.cloned.1.call-update) | async-done | bytes 262160 | tf_op jit(solution)/shard_map/psum | solution.py:41
  1031.0 13.3 psum.84
  1044.4 5.8 cholesky.122
  1051.5 4.9 custom-call.14
  1061.4 42.8 %all-reduce.15.cloned.1.call-done = bf16[640,64]{0,1:T(8,128)(2,1)} async-done(((bf16[640,64]{0,1:T(8,128)(2,1)}), bf16[640,64]{0,1:T(8,128)(2,1)}) %all-reduce.15.cloned.1.call-update) | async-done | bytes 81936 | tf_op jit(solution)/shard_map/psum | solution.py:29
  1105.3 246.0 %psum.86 = f32[64,64]{0,1:T(8,128)S(1)} all-reduce(f32[64,64]{0,1:T(8,128)S(1)} %fusion.53), channel_id=1, replica_groups=mesh['samp'=64,'snp'=4] {'samp'}, use_global_device_ids=true, to_apply=%region_13.17 | all-reduce | flops 4096 | bytes 32768 | tf_op jit(solution)/shard_map/psum | solution.py:30
  1351.4 5.8 cholesky.133
  1358.6 4.9 custom-call.15
  1365.9 176.2 %all-reduce.17.cloned.1.call-done = f32[1024,64]{0,1:T(8,128)} async-done(((f32[1024,64]{0,1:T(8,128)}), f32[1024,64]{0,1:T(8,128)}) %all-reduce.17.cloned.1.call-update) | async-done | bytes 262160 | tf_op jit(solution)/shard_map/psum | solution.py:41
  (95 shorter events, 39.4 us)
Async XLA Ops:
  7.2 32.2 %copy-start = (bf16[1024,64]{0,1:T(8,128)(2,1)S(1)}, bf16[1024,64]{0,1:T(8,128)(2,1)}, u32[]{:S(2)}) copy-start(bf16[1024,64]{0,1:T(8,128)(2,1)} %param.19) | copy-start | bytes 393220
  7.2 14.9 copy-start.6
  7.2 15.2 copy-start.7
  7.2 15.2 copy-start.8
  9.0 23.6 %all-to-all-start = ((f32[64,1,320]{2,1,0:T(1,128)}), f32[64,1,320]{2,1,0:T(1,128)S(1)}, u32[]{:S(2)}, u32[]{:S(2)}) async-start(f32[64,1,320]{2,1,0:T(1,128)} %reshape.78), calls=%async_computation | async-start | bytes 196608 | tf_op jit(solution)/shard_map/all_to_all | solution.py:64
  22.0 56.8 %all-reduce.7.cloned.1.call-start = ((), (), s32[]{:S(2)}) async-start(), calls=%async_computation.1 | async-start | bytes 163840 | tf_op jit(solution)/shard_map/psum | solution.py:29
  22.6 2.2 copy-start.4
  22.6 11.6 copy-start.3
  22.6 11.6 copy-start.5
  40.6 476.0 %all-reduce.9.cloned.1.call-start = ((), (), s32[]{:S(2)}) async-start(), calls=%async_computation.2 | async-start | bytes 524288 | tf_op jit(solution)/shard_map/psum | solution.py:41
  340.4 251.0 %all-reduce.11.cloned.1.call-start = ((), (), s32[]{:S(2)}) async-start(), calls=%async_computation.3 | async-start | bytes 163840 | tf_op jit(solution)/shard_map/psum | solution.py:29
  548.5 481.0 %all-reduce.13.cloned.1.call-start = ((), (), s32[]{:S(2)}) async-start(), calls=%async_computation.4 | async-start | bytes 524288 | tf_op jit(solution)/shard_map/psum | solution.py:41
  853.2 251.0 %all-reduce.15.cloned.1.call-start = ((), (), s32[]{:S(2)}) async-start(), calls=%async_computation.5 | async-start | bytes 163840 | tf_op jit(solution)/shard_map/psum | solution.py:29
  1060.1 305.7 %copy-start.1 = (f32[1024,64]{0,1:T(8,128)}, f32[1024,64]{0,1:T(8,128)S(1)}, u32[]{:S(2)}) copy-start(f32[1024,64]{0,1:T(8,128)S(1)} %rev.23) | copy-start | bytes 786436
  1061.3 480.8 %all-reduce.17.cloned.1.call-start = ((), (), s32[]{:S(2)}) async-start(), calls=%async_computation.6 | async-start | bytes 524288 | tf_op jit(solution)/shard_map/psum | solution.py:41
  1364.8 179.0 %copy-start.2 = (f32[640,64]{0,1:T(8,128)}, f32[640,64]{0,1:T(8,128)S(1)}, u32[]{:S(2)}) copy-start(f32[640,64]{0,1:T(8,128)S(1)} %convolution_bitcast_fusion.2) | copy-start | bytes 491524
Sparse Core Ops, SparseCore 0:
  40.7 38.0 all-reduce.6
  340.6 175.9 all-reduce.8
  548.6 42.7 all-reduce.10
  853.3 176.1 all-reduce.12
  1061.5 42.7 all-reduce.14
  1366.0 176.0 all-reduce.16
